TPU v7x, 512 devices: a whole 4x4x16 slice. The times are simulated.
512 devices in a mesh: stream: 32 (over z, x_hi), span: 16 (over y, x_lo, core).
Axes of the slice: x: 4 (x_hi: 2, x_lo: 2; x = x_hi * 2 + x_lo), y: 4, z: 16, core: 2. Of those that a mesh axis runs over, the one named last changes fastest.
Arguments:
- checkpoint: float32 [5, 192, 32, 2048], P(None, None, 'stream', 'span'), may hold values from -4.8 to 4.8
- adjoint: float32 [5, 192, 32, 2048], P(None, None, 'stream', 'span'), may hold values from -6 to 6
- line_inverse: bfloat16 [32, 3, 320, 320], P('stream'), may hold values from -0.3125 to 0.3125
- row_source: int32 [3072], replicated, may hold values from 0 to 3071, as said below
Outputs:
- adjoint_start: float32 [5, 192, 32, 2048], P(None, None, 'stream', 'span')
Inputs may be any that keep to these rules, and one draw needn't show every extreme that they name: `row_source`: every rotor outlet row is taken by exactly one stator inlet row, and each stator span tile takes exactly 12 rows from each rotor span tile.
All inputs are finite; a program needn't handle non-finite values.
Results may differ from a plain program's by a relative error of at most 0.0029.
Values sent between devices are 32-bit elements; how exact they have to be, the bound alone decides.
A program may use at most 64 MiB of HBM per device.

v0:
```python
import jax
import jax.numpy as jnp
from jax import lax
from jax.sharding import PartitionSpec as P

time_step = 0.5
ADVECTION = (1.0, 0.6, 0.8, 1.2, 0.7)
DISSIPATION = (0.3, 0.25, 0.35, 0.3, 0.4)
SPREADING = (0.4, 0.3, 0.5, 0.35, 0.45)


def with_halo(block, sides, width):
    for axis, dim in sides:
        count = lax.axis_size(axis)
        forward = [(i, i + 1) for i in range(count - 1)]
        forward.append((count - 1, 0))
        backward = [(target, source) for source, target in forward]
        low = lax.ppermute(
            lax.slice_in_dim(block, block.shape[dim] - width, None, axis=dim), axis, forward
        )
        high = lax.ppermute(lax.slice_in_dim(block, 0, width, axis=dim), axis, backward)
        block = jnp.concatenate([low, block, high], axis=dim)
    return block


def per_state(values):
    return jnp.array(values, jnp.float32).reshape(5, 1, 1, 1)


def plane_remap(lower_rim, upper_rim, row_source):
    span_count = lax.axis_size("span")
    position = lax.axis_index("span")
    line_points = lower_rim.shape[1]
    capacity = line_points // span_count
    src_dev = (row_source // line_points).reshape(span_count, line_points)
    src_row = (row_source % line_points).reshape(span_count, line_points)
    devices = jnp.arange(span_count, dtype=jnp.int32)
    slot_ids = jnp.arange(capacity, dtype=jnp.int32)
    point_ids = jnp.arange(line_points, dtype=jnp.int32)
    onehot = (src_dev[:, :, None] == devices[None, None, :]).astype(jnp.int32)
    arrival = jnp.sum((jnp.cumsum(onehot, axis=1) - onehot) * onehot, axis=2)
    pick_lower = (
        (src_dev == position)[:, :, None] & (arrival[:, :, None] == slot_ids[None, None, :])
    ).astype(jnp.int32)
    send_lower = jnp.sum(pick_lower * src_row[:, :, None], axis=1).reshape(span_count * capacity)
    own_dev = lax.dynamic_index_in_dim(src_dev, position, 0, keepdims=False)
    own_arrival = lax.dynamic_index_in_dim(arrival, position, 0, keepdims=False)
    pick_upper = (
        (own_dev[None, :] == devices[:, None])[:, :, None]
        & (own_arrival[None, :, None] == slot_ids[None, None, :])
    ).astype(jnp.int32)
    send_upper = jnp.sum(pick_upper * point_ids[None, :, None], axis=1).reshape(
        span_count * capacity
    )
    outgoing = (jnp.take(lower_rim, send_lower, axis=1), jnp.take(upper_rim, send_upper, axis=1))
    got_lower, got_upper = (
        lax.all_to_all(outgoing[0], "span", split_axis=1, concat_axis=1, tiled=True),
        lax.all_to_all(outgoing[1], "span", split_axis=1, concat_axis=1, tiled=True),
    )
    lower_mapped = jnp.take(got_lower, own_dev * capacity + own_arrival, axis=1)
    matches = (
        (src_dev == position)[:, :, None] & (src_row[:, :, None] == point_ids[None, None, :])
    ).astype(jnp.int32)
    where_from = devices[:, None] * capacity + arrival
    upper_pos = jnp.sum(matches * where_from[:, :, None], axis=(0, 1))
    upper_mapped = jnp.take(got_upper, upper_pos, axis=1)
    return (lower_mapped, upper_mapped)


def gather_rims(field, row_source):
    stream_count = lax.axis_size("stream")
    stream_place = lax.axis_index("stream")
    halfway = stream_count // 2
    padded = with_halo(field, (("stream", 2), ("span", 3)), 1)
    lower_rim = padded[:, :, 0, 1:-1]
    upper_rim = padded[:, :, -1, 1:-1]
    left_rim = padded[:, :, 1:-1, :-2]
    right_rim = padded[:, :, 1:-1, 2:]
    lower_rim = jnp.where(stream_place == 0, 0.0, lower_rim)
    upper_rim = jnp.where(stream_place == stream_count - 1, 0.0, upper_rim)
    lower_mapped, upper_mapped = plane_remap(lower_rim, upper_rim, row_source)
    lower_rim = jnp.where(stream_place == halfway, lower_mapped, lower_rim)
    upper_rim = jnp.where(stream_place == halfway - 1, upper_mapped, upper_rim)
    return (lower_rim, upper_rim, left_rim, right_rim)


def apply_operator(field, rims, coef_down, coef_up, center, lateral):
    lower_rim, upper_rim, left_rim, right_rim = rims
    upstream = jnp.concatenate([lower_rim[:, :, None], field[:, :, :-1]], axis=2)
    downstream = jnp.concatenate([field[:, :, 1:], upper_rim[:, :, None]], axis=2)
    lateral_sum = left_rim + right_rim - 2.0 * field
    return coef_down * downstream + coef_up * upstream + center * field + lateral * lateral_sum


def local(checkpoint, adjoint, line_inverse, row_source):
    advect = per_state(ADVECTION)
    dissip = per_state(DISSIPATION)
    lateral = per_state(SPREADING)
    toward_down = -0.5 * advect + dissip
    toward_up = 0.5 * advect + dissip
    center = -2.0 * dissip
    flux = jnp.tanh(checkpoint)
    flux_rims = gather_rims(flux, row_source)
    advanced = checkpoint + time_step * apply_operator(
        flux, flux_rims, toward_down, toward_up, center, lateral
    )
    tanh_adv = jnp.tanh(advanced)
    section_slope = 2.0 - tanh_adv * tanh_adv
    line_points = checkpoint.shape[1]
    stations = checkpoint.shape[2]
    span_cells = checkpoint.shape[3]
    blocks = line_inverse.shape[1]
    block_points = line_points // blocks
    rounded = adjoint.astype(jnp.bfloat16).reshape(5, blocks, block_points, stations, span_cells)
    inverse = line_inverse.reshape(stations, blocks, 5, block_points, 5, block_points)
    carried = jnp.einsum(
        "sbclem,cblsp->ebmsp", inverse, rounded, preferred_element_type=jnp.float32
    ).reshape(5, line_points, stations, span_cells)
    weighted = section_slope * carried
    weight_rims = gather_rims(weighted, row_source)
    tangent = 1.0 - flux * flux
    return weighted + time_step * tangent * apply_operator(
        weighted, weight_rims, toward_up, toward_down, center, lateral
    )


def solution(mesh):
    return jax.shard_map(
        local,
        mesh=mesh,
        in_specs=(
            P(None, None, "stream", "span"),
            P(None, None, "stream", "span"),
            P("stream", None, None, None),
            P(),
        ),
        out_specs=P(None, None, "stream", "span"),
        check_vma=False,
    )
```

profile of v0, /device:TPU:4, one launch (start us, length us, event | category | flops | bytes accessed | tf_op | source)
XLA Modules:
  0.0 159.7 jit_solution(2668991006154800796)
XLA Ops:
  0.0 1.9 %tanh_bitcast_fusion = (f32[5,192,1,128]{3,1,2,0:T(8,128)}, f32[5,192,1,128]{3,1,0,2:T(8,128)S(1)}) fusion(f32[5,192,1,128]{3,1,0,2:T(8,128)} %bitcast.151), kind=kLoop, calls=%fused_computation.113 | loop fusion | bytes 1474560 | tf_op jit(solution)/shard_map/tanh | solution.py:102
  1.9 7.8 %collective-permute-start = (f32[5,192,1,128]{3,1,2,0:T(8,128)}, f32[5,192,1,128]{3,1,2,0:T(8,128)S(1)}, u32[]{:S(2)}, u32[]{:S(2)}) collective-permute-start(f32[5,192,1,128]{3,1,2,0:T(8,128)} %get-tuple-element.12), channel_id=1, source_target_pairs={{16,0},{32,16},{48,32},{64,48},{80,64},{96,80},{112,96},{128,112},... | collective-permute-start | bytes 1474568 | tf_op jit(solution)/shard_map/ppermute | solution.py:21
  9.7 1.9 %collective-permute-start.1 = (f32[5,192,1,128]{3,1,2,0:T(8,128)}, f32[5,192,1,128]{3,1,2,0:T(8,128)S(1)}, u32[]{:S(2)}, u32[]{:S(2)}) collective-permute-start(f32[5,192,1,128]{3,1,2,0:T(8,128)} %get-tuple-element.12), channel_id=1, source_target_pairs={{0,16},{16,32},{32,48},{48,64},{64,80},{80,96},{96,112},{112,128},... | collective-permute-start | bytes 1474568 | tf_op jit(solution)/shard_map/ppermute | solution.py:18
  11.9 9.1 %reduce-window.6 = s32[16,16,2,128]{3,1,2,0:T(8,128)S(1)} reduce-window(s32[16,16,2,128]{3,1,2,0:T(8,128)S(1)} %copy_bitcast_fusion, s32[]{:T(128)} %constant.84.clone.1), window={size=1x1x1x128 pad=0_0x0_0x0_0x127_0}, to_apply=%region_0.1 | reduce-window | flops 8323072 | bytes 524292 | tf_op jit(solution)/shard_map/reduce-window
  22.8 2.5 %reshape.161 = bf16[3,5,64,5,64]{4,3,2,1,0:T(8,128)(2,1)S(1)} reshape(bf16[1,3,320,320]{3,2,1,0:T(8,128)(2,1)} %param.11) | data formatting | bytes 1228800 | tf_op jit(solution)/shard_map/reshape.24
  25.3 1.4 convert_element_type.6
  26.6 0.7 copy.179
  27.5 1.7 %select_reduce_fusion = s32[192]{0:T(256)S(1)} fusion(s32[16,192]{1,0:T(8,128)S(1)} %broadcast_add_fusion, s32[16,192]{1,0:T(8,128)S(1)} %eq.175, pred[16,192]{1,0:T(8,128)(4,1)S(1)} %broadcast_compare_fusion), kind=kLoop, calls=%fused_computation.8 | loop fusion | flops 2359104 | bytes 28416 | tf_op jit(solution)/shard_map/reduce_sum | solution.py:65
  29.2 2.2 %fusion.3 = f32[5,3,64,1,128]{4,2,0,1,3:T(8,128)} fusion(bf16[3,5,64,5,64]{4,3,2,1,0:T(8,128)(2,1)S(1)} %reshape.161, bf16[5,3,64,128,1]{3,2,1,0,4:T(8,128)(2,1)} %bitcast.159), kind=kOutput, calls=%fused_computation.15 | convolution fusion | flops 78643200 | bytes 1351680 | tf_op jit(solution)/shard_map/sbclem,cblsp->ebmsp/dot_general | solution.py:116
  31.8 0.9 gather_fusion.2
  32.7 1.2 select_bitcast_fusion.2
  33.9 3.7 %all-to-all-start.1 = ((f32[5,192,128]{2,0,1:T(8,128)}), f32[5,192,128]{2,0,1:T(8,128)S(1)}, u32[]{:S(2)}, u32[]{:S(2)}) async-start(f32[5,192,128]{2,0,1:T(8,128)} %select_bitcast_fusion.2), calls=%async_computation.1 | async-start | bytes 1572864 | tf_op jit(solution)/shard_map/all_to_all | solution.py:57
  38.0 1.8 %gather_fusion = f32[192,5,128]{2,1,0:T(8,128)} fusion(f32[5,192,128]{2,0,1:T(8,128)S(1)} %copy.140, s32[1024]{0:T(1024)S(1)} %pad_clamp_fusion.3), kind=kCustom, calls=%fused_computation.clone | custom fusion | bytes 983808 | tf_op jit(solution)/shard_map/jit(_take)/gather | solution.py:55
  39.8 2.3 %select_bitcast_fusion.3 = f32[5,192,128]{2,0,1:T(8,128)} fusion(f32[192,5,128]{2,1,0:T(8,128)} %gather_fusion, pred[192]{0:T(512)(128)(4,1)S(1)} %compare_and_fusion.3), kind=kLoop, calls=%fused_computation.19 | loop fusion | flops 122880 | bytes 983232 | tf_op jit(solution)/shard_map/jit(_take)/select_n | solution.py:55
  42.1 9.3 %all-to-all-done.1 = f32[5,192,128]{2,0,1:T(8,128)S(1)} async-done(((f32[5,192,128]{2,0,1:T(8,128)}), f32[5,192,128]{2,0,1:T(8,128)S(1)}, u32[]{:S(2)}, u32[]{:S(2)}) %all-to-all-start.1) | async-done | bytes 491552 | tf_op jit(solution)/shard_map/all_to_all | solution.py:57
  51.4 4.3 %all-to-all-start = ((f32[5,192,128]{2,0,1:T(8,128)}), f32[5,192,128]{2,0,1:T(8,128)}, u32[]{:S(2)}, u32[]{:S(2)}) async-start(f32[5,192,128]{2,0,1:T(8,128)} %select_bitcast_fusion.3), calls=%async_computation | async-start | bytes 1572864 | tf_op jit(solution)/shard_map/all_to_all | solution.py:58
  55.8 0.5 fusion.39
  56.3 0.6 copy.151
  56.9 5.6 %collective-permute-start.3 = (f32[5,192,3,1]{1,3,2,0:T(1,128)S(1)}, f32[5,192,3,1]{1,3,2,0:T(1,128)S(1)}, u32[]{:S(2)}, u32[]{:S(2)}) collective-permute-start(f32[5,192,3,1]{1,3,2,0:T(1,128)S(1)} %copy.151), channel_id=1, source_target_pairs={{1,0},{2,1},{3,2},{4,3},{5,4},{6,5},{7,6},{8,7},{9,8},{10,9},{11,1... | collective-permute-start | bytes 34568 | tf_op jit(solution)/shard_map/ppermute | solution.py:21
  62.5 0.6 copy.149
  63.1 1.9 %collective-permute-start.2 = (f32[5,192,3,1]{1,3,2,0:T(1,128)S(1)}, f32[5,192,3,1]{1,3,2,0:T(1,128)S(1)}, u32[]{:S(2)}, u32[]{:S(2)}) collective-permute-start(f32[5,192,3,1]{1,3,2,0:T(1,128)S(1)} %copy.149), channel_id=1, source_target_pairs={{0,1},{1,2},{2,3},{3,4},{4,5},{5,6},{6,7},{7,8},{8,9},{9,10},{10,1... | collective-permute-start | bytes 34568 | tf_op jit(solution)/shard_map/ppermute | solution.py:18
  65.1 0.8 copy.158
  65.9 0.5 copy.152
  66.5 3.8 %collective-permute-done.2 = f32[5,192,3,1]{1,3,2,0:T(1,128)S(1)} collective-permute-done((f32[5,192,3,1]{1,3,2,0:T(1,128)S(1)}, f32[5,192,3,1]{1,3,2,0:T(1,128)S(1)}, u32[]{:S(2)}, u32[]{:S(2)}) %collective-permute-start.2) | collective-permute-done | bytes 11552 | tf_op jit(solution)/shard_map/ppermute | solution.py:18
  70.8 2.7 %gather_fusion.3 = f32[192,5,128]{2,1,0:T(8,128)} fusion(f32[5,192,128]{2,0,1:T(8,128)} %copy-done.6, s32[1024]{0:T(1024)S(1)} %pad_clamp_fusion), kind=kCustom, calls=%fused_computation.3.clone | custom fusion | bytes 983808 | tf_op jit(solution)/shard_map/jit(_take)/gather | solution.py:60
  73.5 2.7 %gather_fusion.1 = f32[192,5,128]{2,1,0:T(8,128)} fusion(f32[5,192,128]{2,0,1:T(8,128)} %all-to-all-done, s32[1024]{0:T(1024)S(1)} %pad_clamp_fusion.2), kind=kCustom, calls=%fused_computation.1.clone | custom fusion | bytes 983808 | tf_op jit(solution)/shard_map/jit(_take)/gather | solution.py:66
  76.3 3.9 %fusion.7 = f32[5,192,1,128]{3,1,2,0:T(8,128)} fusion(f32[5,192,1,128]{3,1,2,0:T(8,128)} %bitcast.158, f32[5,192,1,128]{3,1,0,2:T(8,128)S(1)} %bitcast.152, f32[5,192,1,128]{3,1,0,2:T(8,128)} %copy-done.1, f32[5,192,3,1]{3,1,0,2:T(8,128)S(1)} %copy.152, f32[5,192,1,128]{3,1,0,2:T(8,128)} %bitcast.155, f32[5,192,1,128]{3,1,0,2:T(8,128)} %bitcast.157, ...), kind=kLoop, calls=%fused_computation.23 | loop fusion | flops 3317760 | bytes 3955668 | tf_op jit(solution)/shard_map/mul | solution.py:119
  80.2 3.2 %collective-permute-start.5 = (f32[5,192,1,128]{3,1,2,0:T(8,128)}, f32[5,192,1,128]{3,1,2,0:T(8,128)S(1)}, u32[]{:S(2)}, u32[]{:S(2)}) collective-permute-start(f32[5,192,1,128]{3,1,2,0:T(8,128)} %fusion.7), channel_id=1, source_target_pairs={{0,16},{16,32},{32,48},{48,64},{64,80},{80,96},{96,112},{112,128},... | collective-permute-start | bytes 1474568 | tf_op jit(solution)/shard_map/ppermute | solution.py:18
  83.4 8.1 %collective-permute-start.4 = (f32[5,192,1,128]{3,1,2,0:T(8,128)}, f32[5,192,1,128]{3,1,2,0:T(8,128)S(1)}, u32[]{:S(2)}, u32[]{:S(2)}) collective-permute-start(f32[5,192,1,128]{3,1,2,0:T(8,128)} %fusion.7), channel_id=1, source_target_pairs={{16,0},{32,16},{48,32},{64,48},{80,64},{96,80},{112,96},{128,112},... | collective-permute-start | bytes 1474568 | tf_op jit(solution)/shard_map/ppermute | solution.py:21
  91.5 17.4 %collective-permute-done.5 = f32[5,192,1,128]{3,1,2,0:T(8,128)S(1)} collective-permute-done((f32[5,192,1,128]{3,1,2,0:T(8,128)}, f32[5,192,1,128]{3,1,2,0:T(8,128)S(1)}, u32[]{:S(2)}, u32[]{:S(2)}) %collective-permute-start.5) | collective-permute-done | bytes 491552 | tf_op jit(solution)/shard_map/ppermute | solution.py:18
  109.2 0.9 gather_fusion.6
  110.1 1.2 select_bitcast_fusion
  111.3 5.0 %all-to-all-start.3 = ((f32[5,192,128]{2,0,1:T(8,128)}), f32[5,192,128]{2,0,1:T(8,128)S(1)}, u32[]{:S(2)}, u32[]{:S(2)}) async-start(f32[5,192,128]{2,0,1:T(8,128)} %select_bitcast_fusion), calls=%async_computation.3 | async-start | bytes 1572864 | tf_op jit(solution)/shard_map/all_to_all | solution.py:57
  116.3 1.2 copy.162
  117.6 1.8 %gather_fusion.4 = f32[192,5,128]{2,1,0:T(8,128)S(1)} fusion(f32[5,192,128]{2,0,1:T(8,128)} %copy.162, s32[1024]{0:T(1024)S(1)} %pad_clamp_fusion.3), kind=kCustom, calls=%fused_computation.4.clone | custom fusion | bytes 983808 | tf_op jit(solution)/shard_map/jit(_take)/gather | solution.py:55
  119.4 1.2 select_bitcast_fusion.1
  120.6 9.4 %all-to-all-done.3 = f32[5,192,128]{2,0,1:T(8,128)S(1)} async-done(((f32[5,192,128]{2,0,1:T(8,128)}), f32[5,192,128]{2,0,1:T(8,128)S(1)}, u32[]{:S(2)}, u32[]{:S(2)}) %all-to-all-start.3) | async-done | bytes 491552 | tf_op jit(solution)/shard_map/all_to_all | solution.py:57
  130.0 4.5 %all-to-all-start.2 = ((f32[5,192,128]{2,0,1:T(8,128)}), f32[5,192,128]{2,0,1:T(8,128)}, u32[]{:S(2)}, u32[]{:S(2)}) async-start(f32[5,192,128]{2,0,1:T(8,128)} %select_bitcast_fusion.1), calls=%async_computation.2 | async-start | bytes 1572864 | tf_op jit(solution)/shard_map/all_to_all | solution.py:58
  134.5 1.1 pad_maximum_fusion.1
  135.7 0.5 fusion.38
  136.2 0.6 copy.170
  136.8 5.4 %collective-permute-start.7 = (f32[5,192,3,1]{1,3,2,0:T(1,128)S(1)}, f32[5,192,3,1]{1,3,2,0:T(1,128)S(1)}, u32[]{:S(2)}, u32[]{:S(2)}) collective-permute-start(f32[5,192,3,1]{1,3,2,0:T(1,128)S(1)} %copy.170), channel_id=1, source_target_pairs={{1,0},{2,1},{3,2},{4,3},{5,4},{6,5},{7,6},{8,7},{9,8},{10,9},{11,1... | collective-permute-start | bytes 34568 | tf_op jit(solution)/shard_map/ppermute | solution.py:21
  142.2 0.6 copy.168
  142.8 1.9 %collective-permute-start.6 = (f32[5,192,3,1]{1,3,2,0:T(1,128)S(1)}, f32[5,192,3,1]{1,3,2,0:T(1,128)S(1)}, u32[]{:S(2)}, u32[]{:S(2)}) collective-permute-start(f32[5,192,3,1]{1,3,2,0:T(1,128)S(1)} %copy.168), channel_id=1, source_target_pairs={{0,1},{1,2},{2,3},{3,4},{4,5},{5,6},{6,7},{7,8},{8,9},{9,10},{10,1... | collective-permute-start | bytes 34568 | tf_op jit(solution)/shard_map/ppermute | solution.py:18
  145.2 4.7 %collective-permute-done.6 = f32[5,192,3,1]{1,3,2,0:T(1,128)S(1)} collective-permute-done((f32[5,192,3,1]{1,3,2,0:T(1,128)S(1)}, f32[5,192,3,1]{1,3,2,0:T(1,128)S(1)}, u32[]{:S(2)}, u32[]{:S(2)}) %collective-permute-start.6) | collective-permute-done | bytes 11552 | tf_op jit(solution)/shard_map/ppermute | solution.py:18
  150.4 2.7 %gather_fusion.7 = f32[192,5,128]{2,1,0:T(8,128)} fusion(f32[5,192,128]{2,0,1:T(8,128)} %copy-done.7, s32[1024]{0:T(1024)S(1)} %pad_clamp_fusion), kind=kCustom, calls=%fused_computation.7.clone | custom fusion | bytes 983808 | tf_op jit(solution)/shard_map/jit(_take)/gather | solution.py:60
  153.2 2.7 %gather_fusion.5 = f32[192,5,128]{2,1,0:T(8,128)} fusion(f32[5,192,128]{2,0,1:T(8,128)} %all-to-all-done.2, s32[1024]{0:T(1024)S(1)} %pad_clamp_fusion.2), kind=kCustom, calls=%fused_computation.5.clone | custom fusion | bytes 983808 | tf_op jit(solution)/shard_map/jit(_take)/gather | solution.py:66
  155.9 3.7 %fusion.20 = f32[5,192,1,128]{3,1,2,0:T(8,128)} fusion(f32[5,192,1,128]{3,1,2,0:T(8,128)} %fusion.7, f32[5,192,3,1]{3,1,2,0:T(8,128)S(1)} %copy.171, f32[5,192,1,128]{3,1,2,0:T(8,128)} %copy-done.5, f32[5,192,1,128]{3,1,2,0:T(8,128)} %copy-done.4, f32[5,192,3,1]{3,1,2,0:T(8,128)S(1)} %copy.169, f32[192,5,128]{2,1,0:T(8,128)} %gather_fusion.7, ...), kind=kLoop, calls=%fused_computation.37 | loop fusion | flops 3317760 | bytes 3464148 | tf_op jit(solution)/shard_map/add | solution.py:122
  (81 shorter events, 4.7 us)
Async XLA Ops:
  0.0 11.6 %copy-start.9 = (s32[3072]{0:T(1024)S(1)}, s32[3072]{0:T(1024)}, u32[]{:S(2)}) copy-start(s32[3072]{0:T(1024)} %param.12) | copy-start | bytes 36868
  1.9 53.7 %copy-start.1 = (f32[5,192,1,128]{3,1,0,2:T(8,128)}, f32[5,192,1,128]{3,1,0,2:T(8,128)S(1)}, u32[]{:S(2)}) copy-start(f32[5,192,1,128]{3,1,0,2:T(8,128)S(1)} %get-tuple-element.13) | copy-start | bytes 1474564
  1.9 35.7 %collective-permute-start = (f32[5,192,1,128]{3,1,2,0:T(8,128)}, f32[5,192,1,128]{3,1,2,0:T(8,128)S(1)}, u32[]{:S(2)}, u32[]{:S(2)}) collective-permute-start(f32[5,192,1,128]{3,1,2,0:T(8,128)} %get-tuple-element.12), channel_id=1, source_target_pairs={{16,0},{32,16},{48,32},{64,48},{80,64},{96,80},{112,96},{128,112},... | collective-permute-start | bytes 1474568 | tf_op jit(solution)/shard_map/ppermute | solution.py:21
  9.7 21.7 %collective-permute-start.1 = (f32[5,192,1,128]{3,1,2,0:T(8,128)}, f32[5,192,1,128]{3,1,2,0:T(8,128)S(1)}, u32[]{:S(2)}, u32[]{:S(2)}) collective-permute-start(f32[5,192,1,128]{3,1,2,0:T(8,128)} %get-tuple-element.12), channel_id=1, source_target_pairs={{0,16},{16,32},{32,48},{48,64},{64,80},{80,96},{96,112},{112,128},... | collective-permute-start | bytes 1474568 | tf_op jit(solution)/shard_map/ppermute | solution.py:18
  31.4 24.2 %copy-start.3 = (f32[5,192,1,128]{3,1,2,0:T(8,128)}, f32[5,192,1,128]{3,1,2,0:T(8,128)S(1)}, u32[]{:S(2)}) copy-start(f32[5,192,1,128]{3,1,2,0:T(8,128)S(1)} %collective-permute-done.1) | copy-start | bytes 1474564
  33.9 17.5 %all-to-all-start.1 = ((f32[5,192,128]{2,0,1:T(8,128)}), f32[5,192,128]{2,0,1:T(8,128)S(1)}, u32[]{:S(2)}, u32[]{:S(2)}) async-start(f32[5,192,128]{2,0,1:T(8,128)} %select_bitcast_fusion.2), calls=%async_computation.1 | async-start | bytes 1572864 | tf_op jit(solution)/shard_map/all_to_all | solution.py:57
  37.6 18.1 %copy-start.2 = (f32[5,192,1,128]{3,1,2,0:T(8,128)}, f32[5,192,1,128]{3,1,2,0:T(8,128)S(1)}, u32[]{:S(2)}) copy-start(f32[5,192,1,128]{3,1,2,0:T(8,128)S(1)} %collective-permute-done) | copy-start | bytes 1474564
  51.4 4.3 %copy-start.6 = (f32[5,192,128]{2,0,1:T(8,128)}, f32[5,192,128]{2,0,1:T(8,128)S(1)}, u32[]{:S(2)}) copy-start(f32[5,192,128]{2,0,1:T(8,128)S(1)} %all-to-all-done.1) | copy-start | bytes 1474564
  51.4 22.1 %all-to-all-start = ((f32[5,192,128]{2,0,1:T(8,128)}), f32[5,192,128]{2,0,1:T(8,128)}, u32[]{:S(2)}, u32[]{:S(2)}) async-start(f32[5,192,128]{2,0,1:T(8,128)} %select_bitcast_fusion.3), calls=%async_computation | async-start | bytes 1572864 | tf_op jit(solution)/shard_map/all_to_all | solution.py:58
  56.3 8.7 %copy-start.8 = (f32[5,3,64,1,128]{4,2,0,1,3:T(8,128)S(1)}, f32[5,3,64,1,128]{4,2,0,1,3:T(8,128)}, u32[]{:S(2)}) copy-start(f32[5,3,64,1,128]{4,2,0,1,3:T(8,128)} %fusion.3) | copy-start | bytes 1474564
  56.9 9.0 %collective-permute-start.3 = (f32[5,192,3,1]{1,3,2,0:T(1,128)S(1)}, f32[5,192,3,1]{1,3,2,0:T(1,128)S(1)}, u32[]{:S(2)}, u32[]{:S(2)}) collective-permute-start(f32[5,192,3,1]{1,3,2,0:T(1,128)S(1)} %copy.151), channel_id=1, source_target_pairs={{1,0},{2,1},{3,2},{4,3},{5,4},{6,5},{7,6},{8,7},{9,8},{10,9},{11,1... | collective-permute-start | bytes 34568 | tf_op jit(solution)/shard_map/ppermute | solution.py:21
  63.1 7.2 %collective-permute-start.2 = (f32[5,192,3,1]{1,3,2,0:T(1,128)S(1)}, f32[5,192,3,1]{1,3,2,0:T(1,128)S(1)}, u32[]{:S(2)}, u32[]{:S(2)}) collective-permute-start(f32[5,192,3,1]{1,3,2,0:T(1,128)S(1)} %copy.149), channel_id=1, source_target_pairs={{0,1},{1,2},{2,3},{3,4},{4,5},{5,6},{6,7},{7,8},{8,9},{9,10},{10,1... | collective-permute-start | bytes 34568 | tf_op jit(solution)/shard_map/ppermute | solution.py:18
  66.4 9.9 %copy-start = (f32[5,192,1,128]{3,2,1,0:T(1,128)S(1)}, f32[5,192,1,128]{3,2,1,0:T(1,128)}, u32[]{:S(2)}) copy-start(f32[5,192,1,128]{3,2,1,0:T(1,128)} %param.9) | copy-start | bytes 1474564
  66.4 9.8 %copy-start.10 = (f32[5]{0:T(128)S(1)}, f32[5]{0:T(128)}, u32[]{:S(2)}) copy-start(f32[5]{0:T(128)} %constant.95.clone) | copy-start | bytes 64
  66.4 9.8 %copy-start.11 = (f32[5]{0:T(128)S(1)}, f32[5]{0:T(128)}, u32[]{:S(2)}) copy-start(f32[5]{0:T(128)} %constant.105) | copy-start | bytes 64
  66.5 9.8 %copy-start.12 = (f32[5]{0:T(128)S(1)}, f32[5]{0:T(128)}, u32[]{:S(2)}) copy-start(f32[5]{0:T(128)} %constant.104) | copy-start | bytes 64
  66.5 9.8 %copy-start.13 = (f32[5]{0:T(128)S(1)}, f32[5]{0:T(128)}, u32[]{:S(2)}) copy-start(f32[5]{0:T(128)} %constant.102) | copy-start | bytes 64
  80.2 28.6 %collective-permute-start.5 = (f32[5,192,1,128]{3,1,2,0:T(8,128)}, f32[5,192,1,128]{3,1,2,0:T(8,128)S(1)}, u32[]{:S(2)}, u32[]{:S(2)}) collective-permute-start(f32[5,192,1,128]{3,1,2,0:T(8,128)} %fusion.7), channel_id=1, source_target_pairs={{0,16},{16,32},{32,48},{48,64},{64,80},{80,96},{96,112},{112,128},... | collective-permute-start | bytes 1474568 | tf_op jit(solution)/shard_map/ppermute | solution.py:18
  83.4 32.9 %collective-permute-start.4 = (f32[5,192,1,128]{3,1,2,0:T(8,128)}, f32[5,192,1,128]{3,1,2,0:T(8,128)S(1)}, u32[]{:S(2)}, u32[]{:S(2)}) collective-permute-start(f32[5,192,1,128]{3,1,2,0:T(8,128)} %fusion.7), channel_id=1, source_target_pairs={{16,0},{32,16},{48,32},{64,48},{80,64},{96,80},{112,96},{128,112},... | collective-permute-start | bytes 1474568 | tf_op jit(solution)/shard_map/ppermute | solution.py:21
  108.9 25.6 %copy-start.4 = (f32[5,192,1,128]{3,1,2,0:T(8,128)}, f32[5,192,1,128]{3,1,2,0:T(8,128)S(1)}, u32[]{:S(2)}) copy-start(f32[5,192,1,128]{3,1,2,0:T(8,128)S(1)} %collective-permute-done.5) | copy-start | bytes 1474564
  111.3 18.7 %all-to-all-start.3 = ((f32[5,192,128]{2,0,1:T(8,128)}), f32[5,192,128]{2,0,1:T(8,128)S(1)}, u32[]{:S(2)}, u32[]{:S(2)}) async-start(f32[5,192,128]{2,0,1:T(8,128)} %select_bitcast_fusion), calls=%async_computation.3 | async-start | bytes 1572864 | tf_op jit(solution)/shard_map/all_to_all | solution.py:57
  116.3 18.2 %copy-start.5 = (f32[5,192,1,128]{3,1,2,0:T(8,128)}, f32[5,192,1,128]{3,1,2,0:T(8,128)S(1)}, u32[]{:S(2)}) copy-start(f32[5,192,1,128]{3,1,2,0:T(8,128)S(1)} %collective-permute-done.4) | copy-start | bytes 1474564
  130.0 4.5 %copy-start.7 = (f32[5,192,128]{2,0,1:T(8,128)}, f32[5,192,128]{2,0,1:T(8,128)S(1)}, u32[]{:S(2)}) copy-start(f32[5,192,128]{2,0,1:T(8,128)S(1)} %all-to-all-done.3) | copy-start | bytes 1474564
  130.0 23.1 %all-to-all-start.2 = ((f32[5,192,128]{2,0,1:T(8,128)}), f32[5,192,128]{2,0,1:T(8,128)}, u32[]{:S(2)}, u32[]{:S(2)}) async-start(f32[5,192,128]{2,0,1:T(8,128)} %select_bitcast_fusion.1), calls=%async_computation.2 | async-start | bytes 1572864 | tf_op jit(solution)/shard_map/all_to_all | solution.py:58
  136.8 8.0 %collective-permute-start.7 = (f32[5,192,3,1]{1,3,2,0:T(1,128)S(1)}, f32[5,192,3,1]{1,3,2,0:T(1,128)S(1)}, u32[]{:S(2)}, u32[]{:S(2)}) collective-permute-start(f32[5,192,3,1]{1,3,2,0:T(1,128)S(1)} %copy.170), channel_id=1, source_target_pairs={{1,0},{2,1},{3,2},{4,3},{5,4},{6,5},{7,6},{8,7},{9,8},{10,9},{11,1... | collective-permute-start | bytes 34568 | tf_op jit(solution)/shard_map/ppermute | solution.py:21
  142.8 7.2 %collective-permute-start.6 = (f32[5,192,3,1]{1,3,2,0:T(1,128)S(1)}, f32[5,192,3,1]{1,3,2,0:T(1,128)S(1)}, u32[]{:S(2)}, u32[]{:S(2)}) collective-permute-start(f32[5,192,3,1]{1,3,2,0:T(1,128)S(1)} %copy.168), channel_id=1, source_target_pairs={{0,1},{1,2},{2,3},{3,4},{4,5},{5,6},{6,7},{7,8},{8,9},{9,10},{10,1... | collective-permute-start | bytes 34568 | tf_op jit(solution)/shard_map/ppermute | solution.py:18
where the time goes:
time: 161 us; the launch traced here: 160 us
  starting transfers between devices  53.3 us (33%)
  waiting for transfers between devices  44.7 us (28%)
  local copies, waits for them, and re-layouts  30.7 us (19%)
  other arithmetic  28.1 us (17%)
  matrix products  2.23 us (1%)
    ppermute x4, starting transfers between devices, with_halo(): lax.ppermute(lax.slice_in_dim(block, 0, width, axis=dim), axis, backward)  26.9 us
    ppermute x4, waiting for transfers between devices, with_halo(): lax.ppermute(lax.slice_in_dim(block, block.shape[dim] - width, None, axis...  25.9 us
    all_to_all x2, waiting for transfers between devices, plane_remap(): lax.all_to_all(outgoing[0], 'span', split_axis=1, concat_axis=1, tiled=True)  18.8 us
    another operation x4, other arithmetic  9.3 us
    ppermute x4, starting transfers between devices, with_halo(): lax.ppermute(lax.slice_in_dim(block, block.shape[dim] - width, None, axis...  8.91 us
    all_to_all x2, starting transfers between devices, plane_remap(): lax.all_to_all(outgoing[1], 'span', split_axis=1, concat_axis=1, tiled=True)  8.73 us
    all_to_all x2, starting transfers between devices, plane_remap(): lax.all_to_all(outgoing[0], 'span', split_axis=1, concat_axis=1, tiled=True)  8.72 us
    gather x2, local copies, waits for them, and re-layouts, plane_remap(): upper_mapped = jnp.take(got_upper, upper_pos, axis=1)  5.49 us
  transfers between devices with their start and end apart: 12, of which 5 were waited for; matrix products, arithmetic and copies ran while one was open for 29% of the time, Pallas kernels for 0%

commit v1 on v0

--- a/solution.py
+++ b/solution.py
@@ -2,6 +2,7 @@
 import jax.numpy as jnp
 from jax import lax
 from jax.sharding import PartitionSpec as P
+from jax.lax import all_to_all, axis_size
 
 time_step = 0.5
 ADVECTION = (1.0, 0.6, 0.8, 1.2, 0.7)
@@ -28,6 +29,13 @@
 
 
 def plane_remap(lower_rim, upper_rim, row_source):
+
+    def press_rounds(sample):
+        block_out = jnp.concatenate(
+            all_to_all(jnp.stack(jnp.split(sample, axis_size("span"), 1), axis=0), "span", 0, 0), 1
+        )
+        return block_out
+
     span_count = lax.axis_size("span")
     position = lax.axis_index("span")
     line_points = lower_rim.shape[1]
@@ -54,7 +62,7 @@
     )
     outgoing = (jnp.take(lower_rim, send_lower, axis=1), jnp.take(upper_rim, send_upper, axis=1))
     got_lower, got_upper = (
-        lax.all_to_all(outgoing[0], "span", split_axis=1, concat_axis=1, tiled=True),
+        press_rounds(outgoing[0]),
         lax.all_to_all(outgoing[1], "span", split_axis=1, concat_axis=1, tiled=True),
     )
     lower_mapped = jnp.take(got_lower, own_dev * capacity + own_arrival, axis=1)

time: 161 us -> 163 us (1.012)
  local copies, waits for them, and re-layouts: 30.7 us -> 37.1 us
  waiting for transfers between devices: 44.7 us -> 41.8 us
  other arithmetic: 28.1 us -> 26.3 us
    reshape x0 -> x2, local copies, waits for them, and re-layouts: none -> 4.39 us  [press_rounds(): jnp.concatenate(all_to_all(jnp.stack(jnp.split(sample, axis_size('span'),...]
    all_to_all x2, waiting for transfers between devices: 18.8 us -> 15.9 us  [press_rounds(): all_to_all(jnp.stack(jnp.split(sample, axis_size('span'), 1), axis=0), 's...]
    another operation x3 -> x7, local copies, waits for them, and re-layouts: 2.49 us -> 4.37 us
    select_n x3, other arithmetic: 2.33 us -> 0.54 us  [plane_remap(): jnp.take(lower_rim, send_lower, axis=1)]
  transfers between devices with their start and end apart: 12 -> 12, of which waited for: 5 -> 5; matrix products, arithmetic and copies ran while one was open for 29% -> 31% of each run, Pallas kernels for 0% -> 0%
where the time goes in v1:
time: 163 us; the launch traced here: 162 us
  starting transfers between devices  53.3 us (33%)
  waiting for transfers between devices  41.8 us (26%)
  local copies, waits for them, and re-layouts  37.1 us (23%)
  other arithmetic  26.3 us (16%)
  matrix products  2.23 us (1%)
    ppermute x4, starting transfers between devices, with_halo(): lax.ppermute(lax.slice_in_dim(block, 0, width, axis=dim), axis, backward)  27.1 us
    ppermute x4, waiting for transfers between devices, with_halo(): lax.ppermute(lax.slice_in_dim(block, block.shape[dim] - width, None, axis...  25.9 us
    all_to_all x2, waiting for transfers between devices, press_rounds(): all_to_all(jnp.stack(jnp.split(sample, axis_size('span'), 1), axis=0), 's...  15.9 us
    another operation x4, other arithmetic  9.3 us
    ppermute x4, starting transfers between devices, with_halo(): lax.ppermute(lax.slice_in_dim(block, block.shape[dim] - width, None, axis...  8.91 us
    all_to_all x2, starting transfers between devices, press_rounds(): all_to_all(jnp.stack(jnp.split(sample, axis_size('span'), 1), axis=0), 's...  8.76 us
    all_to_all x2, starting transfers between devices, plane_remap(): lax.all_to_all(outgoing[1], 'span', split_axis=1, concat_axis=1, tiled=True)  8.57 us
    gather x2, local copies, waits for them, and re-layouts, plane_remap(): upper_mapped = jnp.take(got_upper, upper_pos, axis=1)  5.47 us
  transfers between devices with their start and end apart: 12, of which 5 were waited for; matrix products, arithmetic and copies ran while one was open for 31% of the time, Pallas kernels for 0%

profile of v1, /device:TPU:4, one launch (start us, length us, event | category | flops | bytes accessed | tf_op | source)
XLA Modules:
  0.0 161.7 jit_solution(13198108812575378885)
XLA Ops:
  0.0 1.9 %tanh_bitcast_fusion = (f32[5,192,1,128]{3,1,2,0:T(8,128)}, f32[5,192,1,128]{3,1,0,2:T(8,128)S(1)}) fusion(f32[5,192,1,128]{3,1,0,2:T(8,128)} %bitcast.283), kind=kLoop, calls=%fused_computation.177 | loop fusion | bytes 1474560 | tf_op jit(solution)/shard_map/tanh | solution.py:110
  1.9 7.8 %collective-permute-start = (f32[5,192,1,128]{3,1,2,0:T(8,128)}, f32[5,192,1,128]{3,1,2,0:T(8,128)S(1)}, u32[]{:S(2)}, u32[]{:S(2)}) collective-permute-start(f32[5,192,1,128]{3,1,2,0:T(8,128)} %get-tuple-element.12), channel_id=1, source_target_pairs={{16,0},{32,16},{48,32},{64,48},{80,64},{96,80},{112,96},{128,112},... | collective-permute-start | bytes 1474568 | tf_op jit(solution)/shard_map/ppermute | solution.py:22
  9.7 1.9 %collective-permute-start.1 = (f32[5,192,1,128]{3,1,2,0:T(8,128)}, f32[5,192,1,128]{3,1,2,0:T(8,128)S(1)}, u32[]{:S(2)}, u32[]{:S(2)}) collective-permute-start(f32[5,192,1,128]{3,1,2,0:T(8,128)} %get-tuple-element.12), channel_id=1, source_target_pairs={{0,16},{16,32},{32,48},{48,64},{64,80},{80,96},{96,112},{112,128},... | collective-permute-start | bytes 1474568 | tf_op jit(solution)/shard_map/ppermute | solution.py:19
  11.9 9.1 %reduce-window.6 = s32[16,16,2,128]{3,1,2,0:T(8,128)S(1)} reduce-window(s32[16,16,2,128]{3,1,2,0:T(8,128)S(1)} %copy_bitcast_fusion, s32[]{:T(128)} %constant.84.clone.1), window={size=1x1x1x128 pad=0_0x0_0x0_0x127_0}, to_apply=%region_0.1 | reduce-window | flops 8323072 | bytes 524292 | tf_op jit(solution)/shard_map/reduce-window
  22.8 2.5 %reshape.175 = bf16[3,5,64,5,64]{4,3,2,1,0:T(8,128)(2,1)S(1)} reshape(bf16[1,3,320,320]{3,2,1,0:T(8,128)(2,1)} %param.11) | data formatting | bytes 1228800 | tf_op jit(solution)/shard_map/reshape.12
  25.3 1.4 convert_element_type.6
  26.6 0.7 copy.211
  27.4 1.7 %select_reduce_fusion = s32[192]{0:T(256)S(1)} fusion(s32[16,192]{1,0:T(8,128)S(1)} %broadcast_add_fusion, s32[16,192]{1,0:T(8,128)S(1)} %eq.175, pred[16,192]{1,0:T(8,128)(4,1)S(1)} %broadcast_compare_fusion), kind=kLoop, calls=%fused_computation.8 | loop fusion | flops 2359104 | bytes 28416 | tf_op jit(solution)/shard_map/reduce_sum | solution.py:73
  29.2 2.2 %fusion.3 = f32[5,3,64,1,128]{4,2,0,1,3:T(8,128)} fusion(bf16[3,5,64,5,64]{4,3,2,1,0:T(8,128)(2,1)S(1)} %reshape.175, bf16[5,3,64,128,1]{3,2,1,0,4:T(8,128)(2,1)} %bitcast.295), kind=kOutput, calls=%fused_computation.15 | convolution fusion | flops 78643200 | bytes 1351680 | tf_op jit(solution)/shard_map/sbclem,cblsp->ebmsp/dot_general | solution.py:124
  31.8 0.9 gather_fusion.2
  33.2 0.9 copy.168
  34.2 3.7 %all-to-all-start.1 = ((f32[16,5,12,128]{3,2,1,0:T(8,128)}), f32[16,5,12,128]{3,2,1,0:T(8,128)S(1)}, u32[]{:S(2)}, u32[]{:S(2)}) async-start(f32[16,5,12,128]{3,2,1,0:T(8,128)} %copy.168), calls=%async_computation.1 | async-start | bytes 1310720 | tf_op jit(solution)/shard_map/all_to_all | solution.py:35
  38.3 1.8 %gather_fusion = f32[192,5,128]{2,1,0:T(8,128)} fusion(f32[5,192,128]{2,0,1:T(8,128)S(1)} %copy.162, s32[1024]{0:T(1024)S(1)} %pad_clamp_fusion.3), kind=kCustom, calls=%fused_computation.clone | custom fusion | bytes 983808 | tf_op jit(solution)/shard_map/jit(_take)/gather | solution.py:63
  40.1 2.3 %select_bitcast_fusion.3 = f32[5,192,128]{2,0,1:T(8,128)} fusion(f32[192,5,128]{2,1,0:T(8,128)} %gather_fusion, pred[192]{0:T(512)(128)(4,1)S(1)} %compare_and_fusion.3), kind=kLoop, calls=%fused_computation.19 | loop fusion | flops 122880 | bytes 983232 | tf_op jit(solution)/shard_map/jit(_take)/select_n | solution.py:63
  42.4 7.9 %all-to-all-done.1 = f32[16,5,12,128]{3,2,1,0:T(8,128)S(1)} async-done(((f32[16,5,12,128]{3,2,1,0:T(8,128)}), f32[16,5,12,128]{3,2,1,0:T(8,128)S(1)}, u32[]{:S(2)}, u32[]{:S(2)}) %all-to-all-start.1) | async-done | bytes 491552 | tf_op jit(solution)/shard_map/all_to_all | solution.py:35
  50.2 4.3 %all-to-all-start = ((f32[5,192,128]{2,0,1:T(8,128)}), f32[5,192,128]{2,0,1:T(8,128)}, u32[]{:S(2)}, u32[]{:S(2)}) async-start(f32[5,192,128]{2,0,1:T(8,128)} %select_bitcast_fusion.3), calls=%async_computation | async-start | bytes 1572864 | tf_op jit(solution)/shard_map/all_to_all | solution.py:66
  54.7 0.5 fusion.39
  55.2 0.6 copy.176
  55.8 5.6 %collective-permute-start.3 = (f32[5,192,3,1]{1,3,2,0:T(1,128)S(1)}, f32[5,192,3,1]{1,3,2,0:T(1,128)S(1)}, u32[]{:S(2)}, u32[]{:S(2)}) collective-permute-start(f32[5,192,3,1]{1,3,2,0:T(1,128)S(1)} %copy.176), channel_id=1, source_target_pairs={{1,0},{2,1},{3,2},{4,3},{5,4},{6,5},{7,6},{8,7},{9,8},{10,9},{11,1... | collective-permute-start | bytes 34568 | tf_op jit(solution)/shard_map/ppermute | solution.py:22
  61.4 0.6 copy.174
  62.0 1.9 %collective-permute-start.2 = (f32[5,192,3,1]{1,3,2,0:T(1,128)S(1)}, f32[5,192,3,1]{1,3,2,0:T(1,128)S(1)}, u32[]{:S(2)}, u32[]{:S(2)}) collective-permute-start(f32[5,192,3,1]{1,3,2,0:T(1,128)S(1)} %copy.174), channel_id=1, source_target_pairs={{0,1},{1,2},{2,3},{3,4},{4,5},{5,6},{6,7},{7,8},{8,9},{9,10},{10,1... | collective-permute-start | bytes 34568 | tf_op jit(solution)/shard_map/ppermute | solution.py:19
  63.9 0.8 copy.183
  65.3 3.9 %collective-permute-done.2 = f32[5,192,3,1]{1,3,2,0:T(1,128)S(1)} collective-permute-done((f32[5,192,3,1]{1,3,2,0:T(1,128)S(1)}, f32[5,192,3,1]{1,3,2,0:T(1,128)S(1)}, u32[]{:S(2)}, u32[]{:S(2)}) %collective-permute-start.2) | collective-permute-done | bytes 11552 | tf_op jit(solution)/shard_map/ppermute | solution.py:19
  69.7 2.2 %copy.205 = f32[5,16,12,128]{3,0,2,1:T(8,128)} copy(f32[5,16,12,128]{3,2,0,1:T(8,128)} %bitcast.290) | data formatting | bytes 983040 | tf_op jit(solution)/shard_map/reshape | solution.py:34
  71.9 2.7 %gather_fusion.3 = f32[192,5,128]{2,1,0:T(8,128)} fusion(f32[5,192,128]{2,0,1:T(8,128)} %bitcast.293, s32[1024]{0:T(1024)S(1)} %get-tuple-element.16), kind=kCustom, calls=%fused_computation.3.clone | custom fusion | bytes 983808 | tf_op jit(solution)/shard_map/jit(_take)/gather | solution.py:68
  74.6 2.7 %gather_fusion.1 = f32[192,5,128]{2,1,0:T(8,128)} fusion(f32[5,192,128]{2,0,1:T(8,128)} %all-to-all-done, s32[1024]{0:T(1024)S(1)} %get-tuple-element.17), kind=kCustom, calls=%fused_computation.1.clone | custom fusion | bytes 983808 | tf_op jit(solution)/shard_map/jit(_take)/gather | solution.py:74
  77.4 3.9 %fusion.7 = f32[5,192,1,128]{3,1,2,0:T(8,128)} fusion(f32[5,192,1,128]{3,1,2,0:T(8,128)} %bitcast.294, f32[5,192,1,128]{3,1,0,2:T(8,128)S(1)} %bitcast.284, f32[5,192,1,128]{3,1,0,2:T(8,128)} %copy-done.1, f32[5,192,3,1]{3,1,0,2:T(8,128)S(1)} %copy.177, f32[5,192,1,128]{3,1,0,2:T(8,128)} %bitcast.287, f32[5,192,1,128]{3,1,0,2:T(8,128)} %bitcast.289, ...), kind=kLoop, calls=%fused_computation.23 | loop fusion | flops 3317760 | bytes 3955668 | tf_op jit(solution)/shard_map/mul | solution.py:127
  81.3 3.2 %collective-permute-start.5 = (f32[5,192,1,128]{3,1,2,0:T(8,128)}, f32[5,192,1,128]{3,1,2,0:T(8,128)S(1)}, u32[]{:S(2)}, u32[]{:S(2)}) collective-permute-start(f32[5,192,1,128]{3,1,2,0:T(8,128)} %fusion.7), channel_id=1, source_target_pairs={{0,16},{16,32},{32,48},{48,64},{64,80},{80,96},{96,112},{112,128},... | collective-permute-start | bytes 1474568 | tf_op jit(solution)/shard_map/ppermute | solution.py:19
  84.5 8.1 %collective-permute-start.4 = (f32[5,192,1,128]{3,1,2,0:T(8,128)}, f32[5,192,1,128]{3,1,2,0:T(8,128)S(1)}, u32[]{:S(2)}, u32[]{:S(2)}) collective-permute-start(f32[5,192,1,128]{3,1,2,0:T(8,128)} %fusion.7), channel_id=1, source_target_pairs={{16,0},{32,16},{48,32},{64,48},{80,64},{96,80},{112,96},{128,112},... | collective-permute-start | bytes 1474568 | tf_op jit(solution)/shard_map/ppermute | solution.py:22
  92.6 17.3 %collective-permute-done.5 = f32[5,192,1,128]{3,1,2,0:T(8,128)S(1)} collective-permute-done((f32[5,192,1,128]{3,1,2,0:T(8,128)}, f32[5,192,1,128]{3,1,2,0:T(8,128)S(1)}, u32[]{:S(2)}, u32[]{:S(2)}) %collective-permute-start.5) | collective-permute-done | bytes 491552 | tf_op jit(solution)/shard_map/ppermute | solution.py:19
  110.3 0.9 gather_fusion.6
  111.7 0.9 copy.191
  112.6 5.0 %all-to-all-start.3 = ((f32[16,5,12,128]{3,2,1,0:T(8,128)}), f32[16,5,12,128]{3,2,1,0:T(8,128)S(1)}, u32[]{:S(2)}, u32[]{:S(2)}) async-start(f32[16,5,12,128]{3,2,1,0:T(8,128)} %copy.191), calls=%async_computation.3 | async-start | bytes 1310720 | tf_op jit(solution)/shard_map/all_to_all | solution.py:35
  117.7 1.2 copy.187
  118.9 1.8 %gather_fusion.4 = f32[192,5,128]{2,1,0:T(8,128)S(1)} fusion(f32[5,192,128]{2,0,1:T(8,128)} %copy.187, s32[1024]{0:T(1024)S(1)} %pad_clamp_fusion.3), kind=kCustom, calls=%fused_computation.4.clone | custom fusion | bytes 983808 | tf_op jit(solution)/shard_map/jit(_take)/gather | solution.py:63
  120.7 1.2 select_bitcast_fusion.1
  121.9 8.0 %all-to-all-done.3 = f32[16,5,12,128]{3,2,1,0:T(8,128)S(1)} async-done(((f32[16,5,12,128]{3,2,1,0:T(8,128)}), f32[16,5,12,128]{3,2,1,0:T(8,128)S(1)}, u32[]{:S(2)}, u32[]{:S(2)}) %all-to-all-start.3) | async-done | bytes 491552 | tf_op jit(solution)/shard_map/all_to_all | solution.py:35
  129.9 4.3 %all-to-all-start.2 = ((f32[5,192,128]{2,0,1:T(8,128)}), f32[5,192,128]{2,0,1:T(8,128)}, u32[]{:S(2)}, u32[]{:S(2)}) async-start(f32[5,192,128]{2,0,1:T(8,128)} %select_bitcast_fusion.1), calls=%async_computation.2 | async-start | bytes 1572864 | tf_op jit(solution)/shard_map/all_to_all | solution.py:66
  134.2 1.1 pad_maximum_fusion.1
  135.9 0.6 copy.198
  136.5 5.6 %collective-permute-start.7 = (f32[5,192,3,1]{1,3,2,0:T(1,128)S(1)}, f32[5,192,3,1]{1,3,2,0:T(1,128)S(1)}, u32[]{:S(2)}, u32[]{:S(2)}) collective-permute-start(f32[5,192,3,1]{1,3,2,0:T(1,128)S(1)} %copy.198), channel_id=1, source_target_pairs={{1,0},{2,1},{3,2},{4,3},{5,4},{6,5},{7,6},{8,7},{9,8},{10,9},{11,1... | collective-permute-start | bytes 34568 | tf_op jit(solution)/shard_map/ppermute | solution.py:22
  142.1 0.6 copy.196
  142.7 1.9 %collective-permute-start.6 = (f32[5,192,3,1]{1,3,2,0:T(1,128)S(1)}, f32[5,192,3,1]{1,3,2,0:T(1,128)S(1)}, u32[]{:S(2)}, u32[]{:S(2)}) collective-permute-start(f32[5,192,3,1]{1,3,2,0:T(1,128)S(1)} %copy.196), channel_id=1, source_target_pairs={{0,1},{1,2},{2,3},{3,4},{4,5},{5,6},{6,7},{7,8},{8,9},{9,10},{10,1... | collective-permute-start | bytes 34568 | tf_op jit(solution)/shard_map/ppermute | solution.py:19
  145.1 4.7 %collective-permute-done.6 = f32[5,192,3,1]{1,3,2,0:T(1,128)S(1)} collective-permute-done((f32[5,192,3,1]{1,3,2,0:T(1,128)S(1)}, f32[5,192,3,1]{1,3,2,0:T(1,128)S(1)}, u32[]{:S(2)}, u32[]{:S(2)}) %collective-permute-start.6) | collective-permute-done | bytes 11552 | tf_op jit(solution)/shard_map/ppermute | solution.py:19
  150.3 2.2 %copy.208 = f32[5,16,12,128]{3,0,2,1:T(8,128)} copy(f32[5,16,12,128]{3,2,0,1:T(8,128)} %bitcast.291) | data formatting | bytes 983040 | tf_op jit(solution)/shard_map/reshape | solution.py:34
  152.5 2.7 %gather_fusion.7 = f32[192,5,128]{2,1,0:T(8,128)} fusion(f32[5,192,128]{2,0,1:T(8,128)} %bitcast.292, s32[1024]{0:T(1024)S(1)} %get-tuple-element.16), kind=kCustom, calls=%fused_computation.7.clone | custom fusion | bytes 983808 | tf_op jit(solution)/shard_map/jit(_take)/gather | solution.py:68
  155.2 2.7 %gather_fusion.5 = f32[192,5,128]{2,1,0:T(8,128)} fusion(f32[5,192,128]{2,0,1:T(8,128)} %all-to-all-done.2, s32[1024]{0:T(1024)S(1)} %get-tuple-element.17), kind=kCustom, calls=%fused_computation.5.clone | custom fusion | bytes 983808 | tf_op jit(solution)/shard_map/jit(_take)/gather | solution.py:74
  158.0 3.7 %fusion.20 = f32[5,192,1,128]{3,1,2,0:T(8,128)} fusion(f32[5,192,1,128]{3,1,2,0:T(8,128)} %fusion.7, f32[5,192,3,1]{3,1,2,0:T(8,128)S(1)} %copy.199, f32[5,192,1,128]{3,1,2,0:T(8,128)} %copy-done.5, f32[5,192,1,128]{3,1,2,0:T(8,128)} %copy-done.4, f32[5,192,3,1]{3,1,2,0:T(8,128)S(1)} %copy.197, f32[192,5,128]{2,1,0:T(8,128)} %gather_fusion.7, ...), kind=kLoop, calls=%fused_computation.37 | loop fusion | flops 3317760 | bytes 3464148 | tf_op jit(solution)/shard_map/add | solution.py:130
  (117 shorter events, 6.5 us)
Async XLA Ops:
  0.0 11.6 %copy-start.9 = (s32[3072]{0:T(1024)S(1)}, s32[3072]{0:T(1024)}, u32[]{:S(2)}) copy-start(s32[3072]{0:T(1024)} %param.12) | copy-start | bytes 36868
  1.9 52.6 %copy-start.1 = (f32[5,192,1,128]{3,1,0,2:T(8,128)}, f32[5,192,1,128]{3,1,0,2:T(8,128)S(1)}, u32[]{:S(2)}) copy-start(f32[5,192,1,128]{3,1,0,2:T(8,128)S(1)} %get-tuple-element.13) | copy-start | bytes 1474564
  1.9 36.0 %collective-permute-start = (f32[5,192,1,128]{3,1,2,0:T(8,128)}, f32[5,192,1,128]{3,1,2,0:T(8,128)S(1)}, u32[]{:S(2)}, u32[]{:S(2)}) collective-permute-start(f32[5,192,1,128]{3,1,2,0:T(8,128)} %get-tuple-element.12), channel_id=1, source_target_pairs={{16,0},{32,16},{48,32},{64,48},{80,64},{96,80},{112,96},{128,112},... | collective-permute-start | bytes 1474568 | tf_op jit(solution)/shard_map/ppermute | solution.py:22
  9.7 21.7 %collective-permute-start.1 = (f32[5,192,1,128]{3,1,2,0:T(8,128)}, f32[5,192,1,128]{3,1,2,0:T(8,128)S(1)}, u32[]{:S(2)}, u32[]{:S(2)}) collective-permute-start(f32[5,192,1,128]{3,1,2,0:T(8,128)} %get-tuple-element.12), channel_id=1, source_target_pairs={{0,16},{16,32},{32,48},{48,64},{64,80},{80,96},{96,112},{112,128},... | collective-permute-start | bytes 1474568 | tf_op jit(solution)/shard_map/ppermute | solution.py:19
  31.5 23.1 %copy-start.3 = (f32[5,192,1,128]{3,1,2,0:T(8,128)}, f32[5,192,1,128]{3,1,2,0:T(8,128)S(1)}, u32[]{:S(2)}) copy-start(f32[5,192,1,128]{3,1,2,0:T(8,128)S(1)} %collective-permute-done.1) | copy-start | bytes 1474564
  34.2 16.1 %all-to-all-start.1 = ((f32[16,5,12,128]{3,2,1,0:T(8,128)}), f32[16,5,12,128]{3,2,1,0:T(8,128)S(1)}, u32[]{:S(2)}, u32[]{:S(2)}) async-start(f32[16,5,12,128]{3,2,1,0:T(8,128)} %copy.168), calls=%async_computation.1 | async-start | bytes 1310720 | tf_op jit(solution)/shard_map/all_to_all | solution.py:35
  37.9 16.6 %copy-start.2 = (f32[5,192,1,128]{3,1,2,0:T(8,128)}, f32[5,192,1,128]{3,1,2,0:T(8,128)S(1)}, u32[]{:S(2)}) copy-start(f32[5,192,1,128]{3,1,2,0:T(8,128)S(1)} %collective-permute-done) | copy-start | bytes 1474564
  50.2 4.3 %copy-start.6 = (f32[16,5,12,128]{3,2,1,0:T(8,128)}, f32[16,5,12,128]{3,2,1,0:T(8,128)S(1)}, u32[]{:S(2)}) copy-start(f32[16,5,12,128]{3,2,1,0:T(8,128)S(1)} %all-to-all-done.1) | copy-start | bytes 1474564
  50.2 24.4 %all-to-all-start = ((f32[5,192,128]{2,0,1:T(8,128)}), f32[5,192,128]{2,0,1:T(8,128)}, u32[]{:S(2)}, u32[]{:S(2)}) async-start(f32[5,192,128]{2,0,1:T(8,128)} %select_bitcast_fusion.3), calls=%async_computation | async-start | bytes 1572864 | tf_op jit(solution)/shard_map/all_to_all | solution.py:66
  55.2 8.7 %copy-start.8 = (f32[5,3,64,1,128]{4,2,0,1,3:T(8,128)S(1)}, f32[5,3,64,1,128]{4,2,0,1,3:T(8,128)}, u32[]{:S(2)}) copy-start(f32[5,3,64,1,128]{4,2,0,1,3:T(8,128)} %fusion.3) | copy-start | bytes 1474564
  55.8 9.0 %collective-permute-start.3 = (f32[5,192,3,1]{1,3,2,0:T(1,128)S(1)}, f32[5,192,3,1]{1,3,2,0:T(1,128)S(1)}, u32[]{:S(2)}, u32[]{:S(2)}) collective-permute-start(f32[5,192,3,1]{1,3,2,0:T(1,128)S(1)} %copy.176), channel_id=1, source_target_pairs={{1,0},{2,1},{3,2},{4,3},{5,4},{6,5},{7,6},{8,7},{9,8},{10,9},{11,1... | collective-permute-start | bytes 34568 | tf_op jit(solution)/shard_map/ppermute | solution.py:22
  62.0 7.2 %collective-permute-start.2 = (f32[5,192,3,1]{1,3,2,0:T(1,128)S(1)}, f32[5,192,3,1]{1,3,2,0:T(1,128)S(1)}, u32[]{:S(2)}, u32[]{:S(2)}) collective-permute-start(f32[5,192,3,1]{1,3,2,0:T(1,128)S(1)} %copy.174), channel_id=1, source_target_pairs={{0,1},{1,2},{2,3},{3,4},{4,5},{5,6},{6,7},{7,8},{8,9},{9,10},{10,1... | collective-permute-start | bytes 34568 | tf_op jit(solution)/shard_map/ppermute | solution.py:19
  69.6 7.7 %copy-start = (f32[5,192,1,128]{3,2,1,0:T(1,128)S(1)}, f32[5,192,1,128]{3,2,1,0:T(1,128)}, u32[]{:S(2)}) copy-start(f32[5,192,1,128]{3,2,1,0:T(1,128)} %param.9) | copy-start | bytes 1474564
  69.6 7.7 %copy-start.10 = (f32[5]{0:T(128)S(1)}, f32[5]{0:T(128)}, u32[]{:S(2)}) copy-start(f32[5]{0:T(128)} %constant.95.clone) | copy-start | bytes 64
  69.7 7.7 %copy-start.11 = (f32[5]{0:T(128)S(1)}, f32[5]{0:T(128)}, u32[]{:S(2)}) copy-start(f32[5]{0:T(128)} %constant.105) | copy-start | bytes 64
  69.7 7.7 %copy-start.12 = (f32[5]{0:T(128)S(1)}, f32[5]{0:T(128)}, u32[]{:S(2)}) copy-start(f32[5]{0:T(128)} %constant.104) | copy-start | bytes 64
  69.7 7.7 %copy-start.13 = (f32[5]{0:T(128)S(1)}, f32[5]{0:T(128)}, u32[]{:S(2)}) copy-start(f32[5]{0:T(128)} %constant.102) | copy-start | bytes 64
  81.3 28.6 %collective-permute-start.5 = (f32[5,192,1,128]{3,1,2,0:T(8,128)}, f32[5,192,1,128]{3,1,2,0:T(8,128)S(1)}, u32[]{:S(2)}, u32[]{:S(2)}) collective-permute-start(f32[5,192,1,128]{3,1,2,0:T(8,128)} %fusion.7), channel_id=1, source_target_pairs={{0,16},{16,32},{32,48},{48,64},{64,80},{80,96},{96,112},{112,128},... | collective-permute-start | bytes 1474568 | tf_op jit(solution)/shard_map/ppermute | solution.py:19
  84.5 33.1 %collective-permute-start.4 = (f32[5,192,1,128]{3,1,2,0:T(8,128)}, f32[5,192,1,128]{3,1,2,0:T(8,128)S(1)}, u32[]{:S(2)}, u32[]{:S(2)}) collective-permute-start(f32[5,192,1,128]{3,1,2,0:T(8,128)} %fusion.7), channel_id=1, source_target_pairs={{16,0},{32,16},{48,32},{64,48},{80,64},{96,80},{112,96},{128,112},... | collective-permute-start | bytes 1474568 | tf_op jit(solution)/shard_map/ppermute | solution.py:22
  109.9 24.3 %copy-start.4 = (f32[5,192,1,128]{3,1,2,0:T(8,128)}, f32[5,192,1,128]{3,1,2,0:T(8,128)S(1)}, u32[]{:S(2)}) copy-start(f32[5,192,1,128]{3,1,2,0:T(8,128)S(1)} %collective-permute-done.5) | copy-start | bytes 1474564
  112.6 17.3 %all-to-all-start.3 = ((f32[16,5,12,128]{3,2,1,0:T(8,128)}), f32[16,5,12,128]{3,2,1,0:T(8,128)S(1)}, u32[]{:S(2)}, u32[]{:S(2)}) async-start(f32[16,5,12,128]{3,2,1,0:T(8,128)} %copy.191), calls=%async_computation.3 | async-start | bytes 1310720 | tf_op jit(solution)/shard_map/all_to_all | solution.py:35
  117.6 16.6 %copy-start.5 = (f32[5,192,1,128]{3,1,2,0:T(8,128)}, f32[5,192,1,128]{3,1,2,0:T(8,128)S(1)}, u32[]{:S(2)}) copy-start(f32[5,192,1,128]{3,1,2,0:T(8,128)S(1)} %collective-permute-done.4) | copy-start | bytes 1474564
  129.9 4.3 %copy-start.7 = (f32[16,5,12,128]{3,2,1,0:T(8,128)}, f32[16,5,12,128]{3,2,1,0:T(8,128)S(1)}, u32[]{:S(2)}) copy-start(f32[16,5,12,128]{3,2,1,0:T(8,128)S(1)} %all-to-all-done.3) | copy-start | bytes 1474564
  129.9 25.3 %all-to-all-start.2 = ((f32[5,192,128]{2,0,1:T(8,128)}), f32[5,192,128]{2,0,1:T(8,128)}, u32[]{:S(2)}, u32[]{:S(2)}) async-start(f32[5,192,128]{2,0,1:T(8,128)} %select_bitcast_fusion.1), calls=%async_computation.2 | async-start | bytes 1572864 | tf_op jit(solution)/shard_map/all_to_all | solution.py:66
  136.5 8.1 %collective-permute-start.7 = (f32[5,192,3,1]{1,3,2,0:T(1,128)S(1)}, f32[5,192,3,1]{1,3,2,0:T(1,128)S(1)}, u32[]{:S(2)}, u32[]{:S(2)}) collective-permute-start(f32[5,192,3,1]{1,3,2,0:T(1,128)S(1)} %copy.198), channel_id=1, source_target_pairs={{1,0},{2,1},{3,2},{4,3},{5,4},{6,5},{7,6},{8,7},{9,8},{10,9},{11,1... | collective-permute-start | bytes 34568 | tf_op jit(solution)/shard_map/ppermute | solution.py:22
  142.7 7.2 %collective-permute-start.6 = (f32[5,192,3,1]{1,3,2,0:T(1,128)S(1)}, f32[5,192,3,1]{1,3,2,0:T(1,128)S(1)}, u32[]{:S(2)}, u32[]{:S(2)}) collective-permute-start(f32[5,192,3,1]{1,3,2,0:T(1,128)S(1)} %copy.196), channel_id=1, source_target_pairs={{0,1},{1,2},{2,3},{3,4},{4,5},{5,6},{6,7},{7,8},{8,9},{9,10},{10,1... | collective-permute-start | bytes 34568 | tf_op jit(solution)/shard_map/ppermute | solution.py:19
